TPU v7x, 512 devices: a whole 4x8x8 slice. The times are simulated.
512 devices in a mesh: shot: 8 (over z_hi, x), recv: 8 (over y), surf: 8 (over z_lo, core).
Axes of the slice: x: 4, y: 8, z: 8 (z_hi: 2, z_lo: 4; z = z_hi * 4 + z_lo), core: 2. Of those that a mesh axis runs over, the one named last changes fastest.
Arguments:
- shot_data: bfloat16 [8, 2, 6144, 2048], P(None, None, ('surf', 'recv'), 'shot'), may hold values from -6 to 6
- recv_data: bfloat16 [8, 2, 6144, 2048], P(None, None, ('surf', 'shot'), 'recv'), may hold values from -0.078125 to 0.078125
- shot_offset: int32 [2048], P('shot'), may hold values from -256 to 255
- recv_offset: int32 [2048], P('recv'), may hold values from -256 to 255
- shot_taper_index: int32 [2048], P('shot'), may hold values from 0 to 3
- receiver_taper_index: int32 [2048], P('recv'), may hold values from 0 to 3
Outputs:
- predicted: float32 [8, 2, 2048, 2048], P('surf', None, 'shot', 'recv')
All inputs are finite; a program needn't handle non-finite values.
Results may differ from a plain program's by a relative error of at most 0.0003.
Values may be sent and summed in bfloat16 or wider, within the bound.
A program may use at most 64 MiB of HBM per device.

v0:
```python
import jax
import jax.numpy as jnp
from jax import lax
from jax.sharding import PartitionSpec as P

R = 2048


def panel_product(left_operand, right_operand):
    real_real = jnp.einsum(
        "xaq,xad->xqd", left_operand[:, 0], right_operand[:, 0], preferred_element_type=jnp.float32
    )
    imag_imag = jnp.einsum(
        "xaq,xad->xqd", left_operand[:, 1], right_operand[:, 1], preferred_element_type=jnp.float32
    )
    real_imag = jnp.einsum(
        "xaq,xad->xqd", left_operand[:, 0], right_operand[:, 1], preferred_element_type=jnp.float32
    )
    imag_real = jnp.einsum(
        "xaq,xad->xqd", left_operand[:, 1], right_operand[:, 0], preferred_element_type=jnp.float32
    )
    return jnp.stack([real_real - imag_imag, real_imag + imag_real], axis=1)


def make_folder(right_full, piece):
    return panel_product(piece, right_full)


def on_device(
    shot_data, recv_data, shot_offset, recv_offset, shot_taper_index, receiver_taper_index
):
    right_full = lax.all_gather(recv_data, "shot", axis=2, tiled=True)
    partial_sum = make_folder(right_full, lax.all_gather(shot_data, "recv", axis=2, tiled=True))
    multiples = lax.psum_scatter(partial_sum, "surf", scatter_dimension=0, tiled=True)
    shot_row_block = shot_offset.shape[0]
    recv_cols = recv_offset.shape[0]
    shot_pos = (
        lax.axis_index("shot") * shot_row_block
        + jnp.arange(shot_row_block, dtype=jnp.int32)
        + shot_offset
    )
    recv_pos = (
        lax.axis_index("recv") * recv_cols + jnp.arange(recv_cols, dtype=jnp.int32) + recv_offset
    )
    distance = jnp.abs(recv_pos[None, :] - shot_pos[:, None])
    half_width = R // 8 * (2 + shot_taper_index[:, None] + receiver_taper_index[None, :])
    ratio = jnp.minimum(distance, half_width).astype(jnp.float32) / half_width.astype(jnp.float32)
    taper = 0.5 * (1.0 + jnp.cos(jnp.pi * ratio))
    return multiples * taper[None, None, :, :]


def solution(mesh):
    placed = (
        P(None, None, ("surf", "recv"), "shot"),
        P(None, None, ("surf", "shot"), "recv"),
        P("shot"),
        P("recv"),
        P("shot"),
        P("recv"),
    )
    return jax.shard_map(
        on_device,
        mesh=mesh,
        in_specs=placed,
        out_specs=P("surf", None, "shot", "recv"),
        check_vma=False,
    )
```

profile of v0, /device:TPU:2, one launch (start us, length us, event | category | flops | bytes accessed | tf_op | source)
XLA Modules:
  0.0 370.5 jit_solution(3620094551108705786)
XLA Ops:
  6.5 0.0 all-gather.3.cloned.1.call-start
  6.5 2.5 copy.10
  9.1 0.0 all-gather.3.cloned.1.call-update
  9.1 0.0 all-gather.5.cloned.1.call-start
  9.1 2.1 copy.12
  11.2 0.0 all-gather.5.cloned.1.call-update
  11.2 0.0 all-reduce.3.cloned.1.call-start
  11.3 79.5 %all-gather.3.cloned.1.call-done = bf16[8,2,768,256]{3,0,1,2:T(8,128)(2,1)} async-done(((bf16[8,2,96,256]{3,0,1,2:T(8,128)(2,1)}), bf16[8,2,768,256]{3,0,1,2:T(8,128)(2,1)}) %all-gather.3.cloned.1.call-update) | async-done | bytes 6291472 | tf_op jit(solution)/shard_map/all_gather | solution.py:33
  90.8 5.9 %fusion.13 = (bf16[8,1,768,256]{3,0,1,2:T(8,128)(2,1)}, bf16[8,1,768,256]{3,0,1,2:T(8,128)(2,1)}) fusion(bf16[8,2,768,256]{3,0,1,2:T(8,128)(2,1)} %all-gather.3.cloned.1.call-done), kind=kLoop, calls=%fused_computation.19 | loop fusion | bytes 12582912 | tf_op jit(solution)/shard_map/slice | solution.py:11
  96.7 3.8 %copy.17 = bf16[8,1,768,256]{2,3,0,1:T(8,128)(2,1)S(1)} copy(bf16[8,1,768,256]{3,0,1,2:T(8,128)(2,1)} %get-tuple-element.5) | data formatting | bytes 6291456
  100.5 5.0 %copy.18 = bf16[8,1,768,256]{2,3,0,1:T(8,128)(2,1)} copy(bf16[8,1,768,256]{3,0,1,2:T(8,128)(2,1)} %get-tuple-element.6) | data formatting | bytes 6291456
  105.5 131.8 %all-gather.5.cloned.1.call-done = bf16[8,2,768,256]{3,2,0,1:T(8,128)(2,1)} async-done(((bf16[8,2,96,256]{3,2,0,1:T(8,128)(2,1)}), bf16[8,2,768,256]{3,2,0,1:T(8,128)(2,1)}) %all-gather.5.cloned.1.call-update) | async-done | bytes 6291472 | tf_op jit(solution)/shard_map/all_gather | solution.py:32
  237.3 0.0 copy-start
  237.3 4.0 %fusion = f32[8,256,256]{2,1,0:T(8,128)S(1)} fusion(bf16[8,1,768,256]{2,3,0,1:T(8,128)(2,1)} %copy.18, bf16[8,2,768,256]{3,2,0,1:T(8,128)(2,1)} %all-gather.5.cloned.1.call-done), kind=kOutput, calls=%fused_computation.3 | convolution fusion | flops 805306368 | bytes 8388608 | tf_op jit(solution)/shard_map/xaq,xad->xqd/dot_general | solution.py:19
  241.3 0.7 copy-done
  242.0 2.9 fusion.2
  244.8 1.0 subtract_bitcast_fusion
  245.8 1.0 add_bitcast_fusion
  246.8 2.3 pad_maximum_fusion
  249.2 0.0 copy-start.4
  249.2 0.0 copy-start.2
  249.2 0.0 copy-start.3
  249.2 0.0 copy-start.1
  249.2 0.0 all-reduce.3.cloned.1.call-update
  249.2 1.3 dynamic-slice
  250.6 0.0 copy-done.4
  250.6 0.0 copy-done.2
  250.6 0.0 copy-done.3
  250.6 0.0 copy-done.1
  250.6 1.1 add_multiply_fusion
  251.7 109.8 %all-reduce.3.cloned.1.call-done = f32[8,2,256,256]{3,2,0,1:T(8,128)} async-done(((f32[8,2,256,256]{3,2,0,1:T(8,128)}), f32[8,2,256,256]{3,2,0,1:T(8,128)}) %all-reduce.3.cloned.1.call-update) | async-done | bytes 4194320
  361.5 2.5 fusion.12
  (2 shorter events, 0.0 us)
Async XLA Ops:
  6.5 84.3 %all-gather.3.cloned.1.call-start = ((), (), s32[]{:S(2)}) async-start(), calls=%async_computation | async-start | bytes 7077888 | tf_op jit(solution)/shard_map/all_gather | solution.py:33
  9.1 228.3 %all-gather.5.cloned.1.call-start = ((), (), s32[]{:S(2)}) async-start(), calls=%async_computation.1 | async-start | bytes 7077888 | tf_op jit(solution)/shard_map/all_gather | solution.py:32
  11.2 350.3 %all-reduce.3.cloned.1.call-start = ((), (), s32[]{:S(2)}) async-start(), calls=%async_computation.2 | async-start | bytes 8388608
  237.3 4.6 %copy-start = (bf16[8,2,768,256]{3,2,0,1:T(8,128)(2,1)S(1)}, bf16[8,2,768,256]{3,2,0,1:T(8,128)(2,1)}, u32[]{:S(2)}) copy-start(bf16[8,2,768,256]{3,2,0,1:T(8,128)(2,1)} %all-gather.5.cloned.1.call-done) | copy-start | bytes 18874372
  249.2 1.4 copy-start.4
  249.2 1.4 copy-start.2
  249.2 1.4 copy-start.3
  249.2 1.4 copy-start.1
Sparse Core Ops, SparseCore 0:
  9.4 81.3 all-gather.2
  93.9 143.3 all-gather.4
  249.3 112.1 all-reduce.2
where the time goes:
time: 371 us
  waiting for transfers between devices  321 us (87%)
  local copies, waits for them, and re-layouts  21.3 us (6%)
  between operations  13.2 us (4%)
  matrix products  8.78 us (2%)
  other arithmetic  5.95 us (2%)
    all_gather x1, waiting for transfers between devices, on_device(): right_full = lax.all_gather(recv_data, 'shot', axis=2, tiled=True)  132 us
    unnamed x4, waiting for transfers between devices  110 us
    all_gather x1, waiting for transfers between devices, on_device(): lax.all_gather(shot_data, 'recv', axis=2, tiled=True)  79.5 us
    unnamed x15, local copies, waits for them, and re-layouts  15.4 us
  transfers between devices with their start and end apart: 3, of which 3 were waited for; matrix products, arithmetic and copies ran while one was open for 5% of the time, Pallas kernels for 0%

commit v1 on v0

--- a/solution.py
+++ b/solution.py
@@ -29,7 +29,9 @@
 def on_device(
     shot_data, recv_data, shot_offset, recv_offset, shot_taper_index, receiver_taper_index
 ):
-    right_full = lax.all_gather(recv_data, "shot", axis=2, tiled=True)
+    right_full = jnp.concatenate(
+        lax.all_to_all(jnp.stack([recv_data] * lax.axis_size("shot")), "shot", 0, 0), axis=2
+    )
     partial_sum = make_folder(right_full, lax.all_gather(shot_data, "recv", axis=2, tiled=True))
     multiples = lax.psum_scatter(partial_sum, "surf", scatter_dimension=0, tiled=True)
     shot_row_block = shot_offset.shape[0]

time: 371 us -> 327 us (0.88)
  waiting for transfers between devices: 321 us -> 251 us
  starting transfers between devices: 0.09 us -> 13.4 us
  local copies, waits for them, and re-layouts: 21.3 us -> 28.2 us
  matrix products: 8.78 us -> 14.2 us
    all_gather x1 -> x0, waiting for transfers between devices: 132 us -> none  [on_device(): right_full = lax.all_gather(recv_data, 'shot', axis=2, tiled=True)]
    all_gather x1, waiting for transfers between devices: 79.5 us -> 0.65 us  [on_device(): lax.all_gather(shot_data, 'recv', axis=2, tiled=True)]
    all_to_all x0 -> x1, waiting for transfers between devices: none -> 72.5 us  [on_device(): lax.all_to_all(jnp.stack([recv_data] * lax.axis_size('shot')), 'shot', 0, 0)]
    unnamed x4 -> x3, waiting for transfers between devices: 110 us -> 178 us
    all_to_all x0 -> x1, starting transfers between devices: none -> 13.4 us  [on_device(): lax.all_to_all(jnp.stack([recv_data] * lax.axis_size('shot')), 'shot', 0, 0)]
    reshape x0 -> x1, local copies, waits for them, and re-layouts: none -> 6.06 us  [on_device(): jnp.concatenate(lax.all_to_all(jnp.stack([recv_data] * lax.axis_size('sho...]
    unnamed x15 -> x23, local copies, waits for them, and re-layouts: 15.4 us -> 12.8 us
  transfers between devices with their start and end apart: 3 -> 3, of which waited for: 3 -> 3; matrix products, arithmetic and copies ran while one was open for 5% -> 3% of each run, Pallas kernels for 0% -> 0%
where the time goes in v1:
time: 327 us; the launch traced here: 326 us
  waiting for transfers between devices  251 us (77%)
  local copies, waits for them, and re-layouts  28.2 us (9%)
  matrix products  14.2 us (4%)
  between operations  13.5 us (4%)
  starting transfers between devices  13.4 us (4%)
  other arithmetic  5.89 us (2%)
    unnamed x3, waiting for transfers between devices  178 us
    all_to_all x1, waiting for transfers between devices, on_device(): lax.all_to_all(jnp.stack([recv_data] * lax.axis_size('shot')), 'shot', 0, 0)  72.5 us
    all_to_all x1, starting transfers between devices, on_device(): lax.all_to_all(jnp.stack([recv_data] * lax.axis_size('shot')), 'shot', 0, 0)  13.4 us
    unnamed x23, local copies, waits for them, and re-layouts  12.8 us
  transfers between devices with their start and end apart: 3, of which 3 were waited for; matrix products, arithmetic and copies ran while one was open for 3% of the time, Pallas kernels for 0%

profile of v1, /device:TPU:2, one launch (start us, length us, event | category | flops | bytes accessed | tf_op | source)
XLA Modules:
  0.0 326.2 jit_solution(2209349870556801867)
XLA Ops:
  6.5 1.2 copy.12
  7.7 3.4 %stack.8 = bf16[8,8,2,96,256]{4,3,1,2,0:T(8,128)(2,1)} broadcast(bf16[8,2,96,256]{3,2,0,1:T(8,128)(2,1)S(1)} %copy.12), dimensions={1,2,3,4} | broadcast | bytes 7077888 | tf_op jit(solution)/shard_map/stack | solution.py:33
  11.2 0.0 copy-start.2
  11.2 13.4 %all-to-all-start = ((bf16[8,8,2,96,256]{4,3,1,2,0:T(8,128)(2,1)}), bf16[8,8,2,96,256]{4,3,1,2,0:T(8,128)(2,1)}, u32[]{:S(2)}, u32[]{:S(2)}) async-start(bf16[8,8,2,96,256]{4,3,1,2,0:T(8,128)(2,1)} %stack.8), calls=%async_computation | async-start | bytes 12582912 | tf_op jit(solution)/shard_map/all_to_all | solution.py:33
  24.6 0.0 all-gather.2.cloned.1.call-start
  24.6 0.0 copy-done.2
  24.6 1.3 copy.10
  25.9 0.0 all-gather.2.cloned.1.call-update
  25.9 0.0 all-reduce.3.cloned.1.call-start
  26.0 72.5 %all-to-all-done = bf16[8,8,2,96,256]{4,3,1,2,0:T(8,128)(2,1)} async-done(((bf16[8,8,2,96,256]{4,3,1,2,0:T(8,128)(2,1)}), bf16[8,8,2,96,256]{4,3,1,2,0:T(8,128)(2,1)}, u32[]{:S(2)}, u32[]{:S(2)}) %all-to-all-start) | async-done | bytes 6291488 | tf_op jit(solution)/shard_map/all_to_all | solution.py:33
  98.5 6.1 %copy.13 = bf16[8,2,8,96,256]{4,3,2,0,1:T(8,128)(2,1)} copy(bf16[8,2,8,96,256]{4,3,0,1,2:T(8,128)(2,1)} %bitcast.1) | data formatting | bytes 12582912 | tf_op jit(solution)/shard_map/reshape | solution.py:32
  104.5 0.7 all-gather.2.cloned.1.call-done
  105.2 5.8 %fusion.13 = (bf16[8,1,768,256]{3,0,1,2:T(8,128)(2,1)}, bf16[8,1,768,256]{3,0,1,2:T(8,128)(2,1)}) fusion(bf16[8,2,768,256]{3,0,1,2:T(8,128)(2,1)} %all-gather.2.cloned.1.call-done), kind=kLoop, calls=%fused_computation.19 | loop fusion | bytes 12582912 | tf_op jit(solution)/shard_map/slice | solution.py:11
  111.0 0.0 slice-start
  111.0 5.3 %copy.19 = bf16[8,1,768,256]{2,3,0,1:T(8,128)(2,1)} copy(bf16[8,1,768,256]{3,0,1,2:T(8,128)(2,1)} %get-tuple-element.6) | data formatting | bytes 6291456
  116.3 0.0 slice-start.1
  116.3 0.0 copy-start
  116.3 5.3 %fusion.2 = f32[8,256,256]{2,1,0:T(8,128)} fusion(bf16[8,1,768,256]{2,3,0,1:T(8,128)(2,1)} %copy.19, bf16[8,2,768,256]{3,2,0,1:T(8,128)(2,1)} %bitcast.41), kind=kOutput, calls=%fused_computation.5 | convolution fusion | flops 805306368 | bytes 8388608 | tf_op jit(solution)/shard_map/xaq,xad->xqd/dot_general | solution.py:13
  121.6 0.0 slice-done
  121.6 0.0 slice-done.1
  121.6 0.0 copy-done
  121.6 2.4 fusion
  124.0 3.8 %copy.18 = bf16[8,1,768,256]{2,3,0,1:T(8,128)(2,1)S(1)} copy(bf16[8,1,768,256]{3,0,1,2:T(8,128)(2,1)} %get-tuple-element.5) | data formatting | bytes 6291456
  127.7 0.0 copy-start.1
  127.8 3.7 %subtract_bitcast_fusion = f32[8,1,256,256]{3,2,0,1:T(8,128)S(1)} fusion(f32[8,256,256]{2,1,0:T(8,128)} %fusion.2, bf16[8,2,768,256]{3,2,0,1:T(8,128)(2,1)} %bitcast.42, bf16[8,1,768,256]{2,3,0,1:T(8,128)(2,1)S(1)} %copy.18), kind=kOutput, calls=%fused_computation.12 | convolution fusion | flops 805830656 | bytes 10485760 | tf_op jit(solution)/shard_map/xaq,xad->xqd/dot_general | solution.py:10
  131.4 0.0 copy-done.1
  131.4 2.9 add_bitcast_fusion
  134.3 2.4 pad_maximum_fusion
  136.7 0.0 copy-start.6
  136.7 0.0 copy-start.4
  136.7 0.0 copy-start.5
  136.7 0.0 copy-start.3
  136.7 0.0 all-reduce.3.cloned.1.call-update
  136.7 1.3 dynamic-slice
  138.0 0.0 copy-done.6
  138.0 0.0 copy-done.4
  138.0 0.0 copy-done.5
  138.0 0.0 copy-done.3
  138.0 1.1 add_multiply_fusion
  139.1 177.8 %all-reduce.3.cloned.1.call-done = f32[8,2,256,256]{3,2,0,1:T(8,128)} async-done(((f32[8,2,256,256]{3,2,0,1:T(8,128)}), f32[8,2,256,256]{3,2,0,1:T(8,128)}) %all-reduce.3.cloned.1.call-update) | async-done | bytes 4194320
  316.9 2.4 fusion.12
  (3 shorter events, 0.0 us)
Async XLA Ops:
  11.2 13.4 %copy-start.2 = (bf16[8,2,96,256]{3,2,1,0:T(8,128)(2,1)S(1)}, bf16[8,2,96,256]{3,2,1,0:T(8,128)(2,1)}, u32[]{:S(2)}) copy-start(bf16[8,2,96,256]{3,2,1,0:T(8,128)(2,1)} %param.6) | copy-start | bytes 2359300
  11.2 87.3 %all-to-all-start = ((bf16[8,8,2,96,256]{4,3,1,2,0:T(8,128)(2,1)}), bf16[8,8,2,96,256]{4,3,1,2,0:T(8,128)(2,1)}, u32[]{:S(2)}, u32[]{:S(2)}) async-start(bf16[8,8,2,96,256]{4,3,1,2,0:T(8,128)(2,1)} %stack.8), calls=%async_computation | async-start | bytes 12582912 | tf_op jit(solution)/shard_map/all_to_all | solution.py:33
  24.6 80.6 %all-gather.2.cloned.1.call-start = ((), (), s32[]{:S(2)}) async-start(), calls=%async_computation.1 | async-start | bytes 7077888 | tf_op jit(solution)/shard_map/all_gather | solution.py:35
  25.9 291.0 %all-reduce.3.cloned.1.call-start = ((), (), s32[]{:S(2)}) async-start(), calls=%async_computation.2 | async-start | bytes 8388608
  111.0 10.6 %slice-start = ((s8[6291456]{0:T(1024)(128)(4,1)}), s8[2097152]{0:T(1024)(128)(4,1)S(1)}, s32[]{:S(2)}) async-start(s8[6291456]{0:T(1024)(128)(4,1)} %bitcast.44), calls=%async_computation.3 | async-start | bytes 4194304
  116.3 5.3 %slice-start.1 = ((s8[6291456]{0:T(1024)(128)(4,1)}), s8[4194304]{0:T(1024)(128)(4,1)S(1)}, s32[]{:S(2)}) async-start(s8[6291456]{0:T(1024)(128)(4,1)} %bitcast.44), calls=%async_computation.4 | async-start | bytes 8388608
  116.3 5.3 %copy-start = (bf16[8,1,768,256]{2,3,0,1:T(8,128)(2,1)S(1)}, bf16[8,1,768,256]{2,3,0,1:T(8,128)(2,1)}, u32[]{:S(2)}) copy-start(bf16[8,1,768,256]{2,3,0,1:T(8,128)(2,1)} %copy.19) | copy-start | bytes 9437188
  127.7 3.7 %copy-start.1 = (f32[8,256,256]{2,1,0:T(8,128)S(1)}, f32[8,256,256]{2,1,0:T(8,128)}, u32[]{:S(2)}) copy-start(f32[8,256,256]{2,1,0:T(8,128)} %fusion) | copy-start | bytes 6291460
  136.7 1.3 copy-start.6
  136.7 1.3 copy-start.4
  136.7 1.3 copy-start.5
  136.7 1.3 copy-start.3
Sparse Core Ops, SparseCore 0:
  27.5 77.6 all-gather.1
  136.8 180.0 all-reduce.2
